TPU v7x, 32 devices: a whole 2x2x4 slice. The times are simulated.
32 devices in a mesh: row: 4 (over z), col: 8 (over y, x, core).
Axes of the slice: x: 2, y: 2, z: 4, core: 2. Of those that a mesh axis runs over, the one named last changes fastest.
Arguments:
- weight: float32 [16384, 16384], P('row', 'col'), may hold values from -0.046875 to 0.046875
- leak: float32 [16384], P('col'), may hold values from 0.1 to 1
- rates: float32 [3, 256, 16384], P(None, 'row', 'col'), may hold values from -0.95 to 0.95
- cotangent: float32 [256, 16384], P('row', 'col'), may hold values from -2 to 2
Outputs:
- grad_input: float32 [256, 16384], P('row', 'col')
- grad_weight: float32 [16384, 16384], P('row', 'col')
- grad_noise: float32 [3, 16384], P(None, 'row')
All inputs are finite; a program needn't handle non-finite values.
Results may differ from a plain program's by a relative error of at most 0.0001.
Values sent between devices are 32-bit elements; how exact they have to be, the bound alone decides.
A program may use at most 192 MiB of HBM per device.

v0:
```python
import jax
import jax.numpy as jnp
from jax import lax
from jax.sharding import PartitionSpec as P

TSTEPS = 3


def shards(weight, leak, rates, cotangent):
    n_col = lax.axis_size("col")
    own_rows = cotangent.shape[0]
    local_units = cotangent.shape[1]
    full_rates = lax.all_gather(rates, "row", axis=1, tiled=True)
    grad_weight = jnp.zeros(weight.shape, jnp.float32)
    noise_list = []
    carried = cotangent
    for step_back in range(TSTEPS - 1, -1, -1):
        scaled = leak[None, :] * carried
        spread = scaled.reshape(own_rows, local_units // n_col, n_col)
        by_col = lax.all_to_all(spread, "col", split_axis=2, concat_axis=1, tiled=True)
        by_row = lax.all_to_all(by_col, "row", split_axis=1, concat_axis=0, tiled=True)
        gathered = lax.all_gather(by_row, "col", axis=2, tiled=True)
        unit_block = gathered.reshape(gathered.shape[0], gathered.shape[1] * gathered.shape[2])
        rates_now = full_rates[step_back]
        noise_list.insert(0, jnp.sum(unit_block, axis=0))
        grad_weight = grad_weight + lax.dot_general(
            unit_block,
            rates_now,
            (((0,), (0,)), ((), ())),
            precision=lax.Precision.HIGHEST,
            preferred_element_type=jnp.float32,
        )
        partial_sum = jnp.dot(
            unit_block, weight, precision=lax.Precision.HIGHEST, preferred_element_type=jnp.float32
        )
        adjoint = lax.psum_scatter(partial_sum, "row", scatter_dimension=0, tiled=True)
        local_rates = rates[step_back]
        carried = (1.0 - leak[None, :]) * carried + (1.0 - local_rates * local_rates) * adjoint
    return (carried, grad_weight, jnp.stack(noise_list))


def solution(mesh):
    placed = (P("row", "col"), P("col"), P(None, "row", "col"), P("row", "col"))
    return jax.shard_map(
        shards,
        mesh=mesh,
        in_specs=placed,
        out_specs=(P("row", "col"), P("row", "col"), P(None, "row")),
        check_vma=False,
    )
```

profile of v0, /device:TPU:0, one launch (start us, length us, event | category | flops | bytes accessed | tf_op | source)
XLA Modules:
  0.0 634.5 jit_solution(5892808969612367369)
XLA Ops:
  7.2 1.1 broadcast_multiply_fusion.2
  8.6 0.4 copy.20
  9.0 14.7 %all_to_all.108 = f32[64,256,8]{1,0,2:T(8,128)S(1)} all-to-all(f32[64,256,8]{1,0,2:T(8,128)S(1)} %copy.20), channel_id=1, replica_groups=mesh['row'=4,'col'=8] {'col'}, dimensions={2} | all-to-all | bytes 1048576 | tf_op jit(solution)/shard_map/all_to_all | solution.py:20
  24.1 0.5 broadcast.24
  24.6 9.3 %reduce.3 = f32[2048,64]{1,0:T(8,128)S(1)} reduce(f32[2048,1,64]{2,1,0:T(1,128)S(1)} %bitcast.75, f32[]{:T(128)} %broadcast.24), dimensions={1}, to_apply=%bitcast.64.reduce_sub_computation | reduce | bytes 1048580
  33.9 0.7 reshape.48
  34.6 18.6 %all_to_all.109 = f32[4,1,32768]{2,1,0:T(1,128)S(1)} all-to-all(f32[4,1,32768]{2,1,0:T(1,128)S(1)} %reshape.48), channel_id=1, replica_groups=mesh['row'=4,'col'=8] {'row'}, dimensions={0} | all-to-all | bytes 1048576 | tf_op jit(solution)/shard_map/all_to_all | solution.py:21
  53.2 2.1 reduce.4
  55.3 1.3 reshape.49
  57.0 1.0 copy.24
  58.3 34.2 %all-gather.5.cloned.1.call-done = f32[256,512,8]{1,0,2:T(8,128)} async-done(((f32[256,512,1]{1,0,2:T(8,128)}), f32[256,512,8]{1,0,2:T(8,128)}) %all-gather.5.cloned.1.call-update) | async-done | bytes 4194320 | tf_op jit(solution)/shard_map/all_gather | solution.py:22
  92.6 5.4 copy.25
  98.0 33.9 %fusion.9 = f32[256,2048]{1,0:T(8,128)} fusion(f32[4096,2048]{1,0:T(8,128)} %param.4, f32[256,512,8]{0,2,1:T(8,128)} %copy.25), kind=kOutput, calls=%fused_computation.10 | convolution fusion | flops 25769803776 | bytes 39845888 | tf_op jit(solution)/shard_map/dot_general | solution.py:33
  132.0 43.7 %reduce-scatter.4.cloned.1.call-done = f32[64,2048]{1,0:T(8,128)} async-done(((f32[256,2048]{1,0:T(8,128)}), f32[64,2048]{1,0:T(8,128)}) %reduce-scatter.4.cloned.1.call-update) | async-done | bytes 524304 | tf_op jit(solution)/shard_map/reduce_scatter | solution.py:36
  175.7 1.3 broadcast_multiply_fusion.1
  177.7 13.7 %all_to_all.110 = f32[64,256,8]{1,0,2:T(8,128)S(1)} all-to-all(f32[64,256,8]{1,0,2:T(8,128)S(1)} %copy.27), channel_id=1, replica_groups=mesh['row'=4,'col'=8] {'col'}, dimensions={2} | all-to-all | bytes 1048576 | tf_op jit(solution)/shard_map/all_to_all | solution.py:20
  191.8 9.3 %reduce.5 = f32[2048,64]{1,0:T(8,128)S(1)} reduce(f32[2048,1,64]{2,1,0:T(1,128)S(1)} %bitcast.76, f32[]{:T(128)} %broadcast.24), dimensions={1}, to_apply=%bitcast.66.reduce_sub_computation | reduce | bytes 1048580
  201.1 0.7 reshape.50
  201.8 16.6 %all_to_all.111 = f32[4,1,32768]{2,1,0:T(1,128)S(1)} all-to-all(f32[4,1,32768]{2,1,0:T(1,128)S(1)} %reshape.50), channel_id=1, replica_groups=mesh['row'=4,'col'=8] {'row'}, dimensions={0} | all-to-all | bytes 1048576 | tf_op jit(solution)/shard_map/all_to_all | solution.py:21
  218.4 2.1 reduce.6
  220.5 1.3 reshape.51
  222.2 1.0 copy.31
  223.4 34.3 %all-gather.7.cloned.1.call-done = f32[256,512,8]{1,0,2:T(8,128)} async-done(((f32[256,512,1]{1,0,2:T(8,128)}), f32[256,512,8]{1,0,2:T(8,128)}) %all-gather.7.cloned.1.call-update) | async-done | bytes 4194320 | tf_op jit(solution)/shard_map/all_gather | solution.py:22
  257.7 5.5 copy.32
  263.2 33.8 %fusion.5 = f32[256,2048]{1,0:T(8,128)} fusion(f32[4096,2048]{1,0:T(8,128)} %param.4, f32[256,512,8]{0,2,1:T(8,128)} %copy.32), kind=kOutput, calls=%fused_computation.6 | convolution fusion | flops 25769803776 | bytes 39845888 | tf_op jit(solution)/shard_map/dot_general | solution.py:33
  297.2 0.5 all-gather.11.cloned.1.call-update
  297.8 43.2 %reduce-scatter.6.cloned.1.call-done = f32[64,2048]{1,0:T(8,128)} async-done(((f32[256,2048]{1,0:T(8,128)}), f32[64,2048]{1,0:T(8,128)}) %reduce-scatter.6.cloned.1.call-update) | async-done | bytes 524304 | tf_op jit(solution)/shard_map/reduce_scatter | solution.py:36
  340.9 2.0 broadcast_multiply_fusion
  343.3 0.4 copy.34
  343.7 13.5 %all_to_all.112 = f32[64,256,8]{1,0,2:T(8,128)} all-to-all(f32[64,256,8]{1,0,2:T(8,128)S(1)} %copy.34), channel_id=1, replica_groups=mesh['row'=4,'col'=8] {'col'}, dimensions={2} | all-to-all | bytes 1048576 | tf_op jit(solution)/shard_map/all_to_all | solution.py:20
  357.2 1.4 copy.47
  358.5 10.3 %reduce.7 = f32[2048,64]{1,0:T(8,128)} reduce(f32[2048,1,64]{2,1,0:T(1,128)S(1)} %bitcast.77, f32[]{:T(128)} %broadcast.24), dimensions={1}, to_apply=%bitcast.68.reduce_sub_computation | reduce | bytes 1048580
  368.9 1.9 reshape.52
  370.7 32.0 %all_to_all.113 = f32[4,1,32768]{2,1,0:T(1,128)S(1)} all-to-all(f32[4,1,32768]{2,1,0:T(1,128)S(1)} %reshape.52), channel_id=1, replica_groups=mesh['row'=4,'col'=8] {'row'}, dimensions={0} | all-to-all | bytes 1048576 | tf_op jit(solution)/shard_map/all_to_all | solution.py:21
  402.7 2.1 reduce.8
  404.8 1.3 reshape.53
  406.5 1.0 copy.38
  407.8 2.6 reduce_sum.29
  410.7 57.2 %all-gather.11.cloned.1.call-done = f32[3,256,2048]{2,1,0:T(8,128)} async-done(((f32[3,64,2048]{2,1,0:T(8,128)}), f32[3,256,2048]{2,1,0:T(8,128)}) %all-gather.11.cloned.1.call-update) | async-done | bytes 6291472 | tf_op jit(solution)/shard_map/all_gather | solution.py:13
  468.0 32.4 %fusion.7 = f32[4096,2048]{1,0:T(8,128)} fusion(f32[256,512,8]{0,2,1:T(8,128)} %copy.25, f32[3,256,2048]{2,1,0:T(8,128)} %all-gather.11.cloned.1.call-done), kind=kOutput, calls=%fused_computation.8 | convolution fusion | flops 25769803776 | bytes 39845888 | tf_op jit(solution)/shard_map/dot_general | solution.py:26
  500.4 2.7 reduce_sum.28
  503.4 32.7 %fusion.3 = f32[4096,2048]{1,0:T(8,128)} fusion(f32[256,512,8]{0,2,1:T(8,128)} %copy.32, f32[3,256,2048]{2,1,0:T(8,128)} %all-gather.11.cloned.1.call-done), kind=kOutput, calls=%fused_computation.4 | convolution fusion | flops 25769803776 | bytes 39845888 | tf_op jit(solution)/shard_map/dot_general | solution.py:26
  536.0 2.6 reduce_sum.27
  539.0 5.5 copy.39
  544.4 33.9 %fusion.1 = f32[256,2048]{1,0:T(8,128)} fusion(f32[4096,2048]{1,0:T(8,128)} %param.4, f32[256,512,8]{0,2,1:T(8,128)} %copy.39), kind=kOutput, calls=%fused_computation.2 | convolution fusion | flops 25769803776 | bytes 39845888 | tf_op jit(solution)/shard_map/dot_general | solution.py:33
  578.4 0.7 pad_maximum_fusion
  579.1 46.4 %add_add_fusion = f32[4096,2048]{1,0:T(8,128)} fusion(f32[4096,2048]{1,0:T(8,128)} %fusion.7, f32[4096,2048]{1,0:T(8,128)} %fusion.3, f32[256,512,8]{0,2,1:T(8,128)} %copy.39, f32[3,256,2048]{2,1,0:T(8,128)} %all-gather.11.cloned.1.call-done), kind=kOutput, calls=%fused_computation | convolution fusion | flops 25786580992 | bytes 106954752 | tf_op jit(solution)/shard_map/dot_general | solution.py:26
  625.4 1.9 fusion.11
  (41 shorter events, 5.1 us)
Async XLA Ops:
  7.2 85.4 %all-gather.5.cloned.1.call-start = ((), (), s32[]{:S(2)}) async-start(), calls=%async_computation.9 | async-start | bytes 4718592 | tf_op jit(solution)/shard_map/all_gather | solution.py:22
  58.0 117.7 %reduce-scatter.4.cloned.1.call-start = ((), (), s32[]{:S(2)}) async-start(), calls=%async_computation.10 | async-start | bytes 2621440 | tf_op jit(solution)/shard_map/reduce_scatter | solution.py:36
  98.0 33.9 %copy-start.4 = (f32[2048]{0:T(1024)S(1)}, f32[2048]{0:T(1024)}, u32[]{:S(2)}) copy-start(f32[2048]{0:T(1024)} %param.5) | copy-start | bytes 24580
  98.0 77.7 %copy-start.1 = (f32[64,2048]{1,0:T(8,128)S(1)}, f32[64,2048]{1,0:T(8,128)}, u32[]{:S(2)}) copy-start(f32[64,2048]{1,0:T(8,128)} %param.7) | copy-start | bytes 1572868
  131.9 125.9 %all-gather.7.cloned.1.call-start = ((), (), s32[]{:S(2)}) async-start(), calls=%async_computation.11 | async-start | bytes 4718592 | tf_op jit(solution)/shard_map/all_gather | solution.py:22
  223.2 117.7 %reduce-scatter.6.cloned.1.call-start = ((), (), s32[]{:S(2)}) async-start(), calls=%async_computation.12 | async-start | bytes 2621440 | tf_op jit(solution)/shard_map/reduce_scatter | solution.py:36
  263.2 77.7 %copy-start.3 = (f32[64,2048]{1,0:T(8,128)S(1)}, f32[64,2048]{1,0:T(8,128)}, u32[]{:S(2)}) copy-start(f32[64,2048]{1,0:T(8,128)} %reduce-scatter.4.cloned.1.call-done) | copy-start | bytes 1572868
  297.1 43.8 %copy-start = (f32[3,64,2048]{2,1,0:T(8,128)S(1)}, f32[3,64,2048]{2,1,0:T(8,128)}, u32[]{:S(2)}) copy-start(f32[3,64,2048]{2,1,0:T(8,128)} %param.6) | copy-start | bytes 4718596
  297.1 170.9 %all-gather.11.cloned.1.call-start = ((), (), s32[]{:S(2)}) async-start(), calls=%async_computation.15 | async-start | bytes 7864320 | tf_op jit(solution)/shard_map/all_gather | solution.py:13
  297.7 238.3 %all-gather.9.cloned.1.call-start = ((), (), s32[]{:S(2)}) async-start(), calls=%async_computation.13 | async-start | bytes 4718592 | tf_op jit(solution)/shard_map/all_gather | solution.py:22
  407.5 217.9 %reduce-scatter.8.cloned.1.call-start = ((), (), s32[]{:S(2)}) async-start(), calls=%async_computation.14 | async-start | bytes 2621440 | tf_op jit(solution)/shard_map/reduce_scatter | solution.py:36
  579.1 46.4 %copy-start.2 = (f32[64,2048]{1,0:T(8,128)S(1)}, f32[64,2048]{1,0:T(8,128)}, u32[]{:S(2)}) copy-start(f32[64,2048]{1,0:T(8,128)} %get-tuple-element.4) | copy-start | bytes 1572868
Sparse Core Ops, SparseCore 0:
  58.1 34.4 all-gather.4
  132.0 43.6 reduce-scatter.3
  223.3 34.4 all-gather.6
  297.2 43.6 reduce-scatter.5
  342.3 125.6 all-gather.10
  469.7 34.7 all-gather.8
  578.5 41.7 reduce-scatter.7
where the time goes:
time: 642 us; the launch traced here: 634 us
  waiting for transfers between devices  213 us (33%)
  matrix products  213 us (33%)
  blocking collectives  109 us (17%)
  other arithmetic  50.4 us (8%)
  local copies, waits for them, and re-layouts  33 us (5%)
  between operations  14.6 us (2%)
    dot_general x3, matrix products, shards(): lax.dot_general(unit_block, rates_now, (((0,), (0,)), ((), ())), precisio...  111 us
    dot_general x3, matrix products, shards(): jnp.dot(unit_block, weight, precision=lax.Precision.HIGHEST, preferred_el...  102 us
    reduce_scatter x3, waiting for transfers between devices, shards(): lax.psum_scatter(partial_sum, 'row', scatter_dimension=0, tiled=True)  86.9 us
    all_gather x3, waiting for transfers between devices, shards(): gathered = lax.all_gather(by_row, 'col', axis=2, tiled=True)  68.6 us
    all_to_all x3, blocking collectives, shards(): lax.all_to_all(by_col, 'row', split_axis=1, concat_axis=0, tiled=True)  67.2 us
    all_gather x1, waiting for transfers between devices, shards(): full_rates = lax.all_gather(rates, 'row', axis=1, tiled=True)  57.2 us
    all_to_all x3, blocking collectives, shards(): lax.all_to_all(spread, 'col', split_axis=2, concat_axis=1, tiled=True)  41.9 us
    unnamed x3, other arithmetic  29 us
  transfers between devices with their start and end apart: 7, of which 5 were waited for; matrix products, arithmetic and copies ran while one was open for 22% of the time, Pallas kernels for 0%

commit v1 on v0

--- a/solution.py
+++ b/solution.py
@@ -17,7 +17,10 @@
     for step_back in range(TSTEPS - 1, -1, -1):
         scaled = leak[None, :] * carried
         spread = scaled.reshape(own_rows, local_units // n_col, n_col)
-        by_col = lax.all_to_all(spread, "col", split_axis=2, concat_axis=1, tiled=True)
+        by_col = jnp.concatenate(
+            lax.all_to_all(jnp.stack(jnp.split(spread, lax.axis_size("col"), axis=2)), "col", 0, 0),
+            axis=1,
+        )
         by_row = lax.all_to_all(by_col, "row", split_axis=1, concat_axis=0, tiled=True)
         gathered = lax.all_gather(by_row, "col", axis=2, tiled=True)
         unit_block = gathered.reshape(gathered.shape[0], gathered.shape[1] * gathered.shape[2])

time: 642 us -> 644 us (level)
  no operation moved by 1% of the time
where the time goes in v1:
time: 644 us; the launch traced here: 636 us
  waiting for transfers between devices  213 us (33%)
  matrix products  213 us (33%)
  blocking collectives  109 us (17%)
  other arithmetic  50.4 us (8%)
  local copies, waits for them, and re-layouts  34.2 us (5%)
  between operations  14.9 us (2%)
    dot_general x3, matrix products, shards(): lax.dot_general(unit_block, rates_now, (((0,), (0,)), ((), ())), precisio...  111 us
    dot_general x3, matrix products, shards(): jnp.dot(unit_block, weight, precision=lax.Precision.HIGHEST, preferred_el...  102 us
    reduce_scatter x3, waiting for transfers between devices, shards(): lax.psum_scatter(partial_sum, 'row', scatter_dimension=0, tiled=True)  86.9 us
    all_gather x3, waiting for transfers between devices, shards(): gathered = lax.all_gather(by_row, 'col', axis=2, tiled=True)  68.3 us
    all_to_all x3, blocking collectives, shards(): lax.all_to_all(by_col, 'row', split_axis=1, concat_axis=0, tiled=True)  67.3 us
    all_gather x1, waiting for transfers between devices, shards(): full_rates = lax.all_gather(rates, 'row', axis=1, tiled=True)  57.2 us
    all_to_all x3, blocking collectives, shards(): lax.all_to_all(jnp.stack(jnp.split(spread, lax.axis_size('col'), axis=2))...  41.5 us
    unnamed x3, other arithmetic  29 us
  transfers between devices with their start and end apart: 7, of which 5 were waited for; matrix products, arithmetic and copies ran while one was open for 22% of the time, Pallas kernels for 0%

profile of v1, /device:TPU:0, one launch (start us, length us, event | category | flops | bytes accessed | tf_op | source)
XLA Modules:
  0.0 635.5 jit_solution(4584358490398067704)
XLA Ops:
  7.2 1.1 broadcast_multiply_fusion.2
  8.6 0.7 fusion.17
  9.8 14.7 %all_to_all.69 = f32[8,64,256,1]{2,1,3,0:T(8,128)S(1)} all-to-all(f32[8,64,256,1]{2,1,3,0:T(8,128)S(1)} %copy.73), channel_id=1, replica_groups=mesh['row'=4,'col'=8] {'col'}, dimensions={0} | all-to-all | bytes 1048576 | tf_op jit(solution)/shard_map/all_to_all | solution.py:21
  25.4 9.3 %reduce.3 = f32[2048,64]{1,0:T(8,128)S(1)} reduce(f32[2048,1,64]{2,1,0:T(1,128)S(1)} %bitcast.129, f32[]{:T(128)} %broadcast.24), dimensions={1}, to_apply=%bitcast.118.reduce_sub_computation | reduce | bytes 1048580
  34.7 0.7 reshape.72
  35.4 18.6 %all_to_all.70 = f32[4,1,32768]{2,1,0:T(1,128)S(1)} all-to-all(f32[4,1,32768]{2,1,0:T(1,128)S(1)} %reshape.72), channel_id=1, replica_groups=mesh['row'=4,'col'=8] {'row'}, dimensions={0} | all-to-all | bytes 1048576 | tf_op jit(solution)/shard_map/all_to_all | solution.py:24
  54.0 2.1 reduce.4
  56.1 1.3 reshape.73
  57.8 1.0 copy.77
  58.8 0.6 reduce-scatter.4.cloned.1.call-start
  59.4 34.0 %all-gather.5.cloned.1.call-done = f32[256,512,8]{1,0,2:T(8,128)} async-done(((f32[256,512,1]{1,0,2:T(8,128)}), f32[256,512,8]{1,0,2:T(8,128)}) %all-gather.5.cloned.1.call-update) | async-done | bytes 4194320 | tf_op jit(solution)/shard_map/all_gather | solution.py:25
  93.4 5.4 copy.78
  98.8 33.9 %fusion.9 = f32[256,2048]{1,0:T(8,128)} fusion(f32[4096,2048]{1,0:T(8,128)} %param.4, f32[256,512,8]{0,2,1:T(8,128)} %copy.78), kind=kOutput, calls=%fused_computation.10 | convolution fusion | flops 25769803776 | bytes 39845888 | tf_op jit(solution)/shard_map/dot_general | solution.py:36
  132.8 43.7 %reduce-scatter.4.cloned.1.call-done = f32[64,2048]{1,0:T(8,128)} async-done(((f32[256,2048]{1,0:T(8,128)}), f32[64,2048]{1,0:T(8,128)}) %reduce-scatter.4.cloned.1.call-update) | async-done | bytes 524304 | tf_op jit(solution)/shard_map/reduce_scatter | solution.py:39
  176.5 1.3 broadcast_multiply_fusion.1
  178.1 0.7 fusion.16
  179.3 13.3 %all_to_all.71 = f32[8,64,256,1]{2,1,3,0:T(8,128)S(1)} all-to-all(f32[8,64,256,1]{2,1,3,0:T(8,128)S(1)} %copy.88), channel_id=1, replica_groups=mesh['row'=4,'col'=8] {'col'}, dimensions={0} | all-to-all | bytes 1048576 | tf_op jit(solution)/shard_map/all_to_all | solution.py:21
  193.0 9.3 %reduce.5 = f32[2048,64]{1,0:T(8,128)S(1)} reduce(f32[2048,1,64]{2,1,0:T(1,128)S(1)} %bitcast.130, f32[]{:T(128)} %broadcast.24), dimensions={1}, to_apply=%bitcast.120.reduce_sub_computation | reduce | bytes 1048580
  202.4 0.7 reshape.74
  203.0 16.6 %all_to_all.72 = f32[4,1,32768]{2,1,0:T(1,128)S(1)} all-to-all(f32[4,1,32768]{2,1,0:T(1,128)S(1)} %reshape.74), channel_id=1, replica_groups=mesh['row'=4,'col'=8] {'row'}, dimensions={0} | all-to-all | bytes 1048576 | tf_op jit(solution)/shard_map/all_to_all | solution.py:24
  219.6 2.1 reduce.6
  221.8 1.3 reshape.75
  223.4 1.0 copy.92
  224.7 34.3 %all-gather.7.cloned.1.call-done = f32[256,512,8]{1,0,2:T(8,128)} async-done(((f32[256,512,1]{1,0,2:T(8,128)}), f32[256,512,8]{1,0,2:T(8,128)}) %all-gather.7.cloned.1.call-update) | async-done | bytes 4194320 | tf_op jit(solution)/shard_map/all_gather | solution.py:25
  259.0 5.5 copy.93
  264.5 33.9 %fusion.5 = f32[256,2048]{1,0:T(8,128)} fusion(f32[4096,2048]{1,0:T(8,128)} %param.4, f32[256,512,8]{0,2,1:T(8,128)} %copy.93), kind=kOutput, calls=%fused_computation.6 | convolution fusion | flops 25769803776 | bytes 39845888 | tf_op jit(solution)/shard_map/dot_general | solution.py:36
  298.4 0.5 all-gather.11.cloned.1.call-update
  299.0 43.2 %reduce-scatter.6.cloned.1.call-done = f32[64,2048]{1,0:T(8,128)} async-done(((f32[256,2048]{1,0:T(8,128)}), f32[64,2048]{1,0:T(8,128)}) %reduce-scatter.6.cloned.1.call-update) | async-done | bytes 524304 | tf_op jit(solution)/shard_map/reduce_scatter | solution.py:39
  342.2 2.0 broadcast_multiply_fusion
  344.5 0.7 fusion.15
  345.7 13.4 %all_to_all.73 = f32[8,64,256,1]{2,1,3,0:T(8,128)S(1)} all-to-all(f32[8,64,256,1]{2,1,3,0:T(8,128)S(1)} %copy.103), channel_id=1, replica_groups=mesh['row'=4,'col'=8] {'col'}, dimensions={0} | all-to-all | bytes 1048576 | tf_op jit(solution)/shard_map/all_to_all | solution.py:21
  359.5 10.3 %reduce.7 = f32[2048,64]{1,0:T(8,128)} reduce(f32[2048,1,64]{2,1,0:T(1,128)S(1)} %bitcast.131, f32[]{:T(128)} %broadcast.24), dimensions={1}, to_apply=%bitcast.122.reduce_sub_computation | reduce | bytes 1048580
  369.8 1.9 reshape.76
  371.7 32.1 %all_to_all.74 = f32[4,1,32768]{2,1,0:T(1,128)S(1)} all-to-all(f32[4,1,32768]{2,1,0:T(1,128)S(1)} %reshape.76), channel_id=1, replica_groups=mesh['row'=4,'col'=8] {'row'}, dimensions={0} | all-to-all | bytes 1048576 | tf_op jit(solution)/shard_map/all_to_all | solution.py:24
  403.7 2.1 reduce.8
  405.9 1.3 reshape.77
  407.6 1.0 copy.107
  409.1 2.6 reduce_sum.29
  412.0 57.2 %all-gather.11.cloned.1.call-done = f32[3,256,2048]{2,1,0:T(8,128)} async-done(((f32[3,64,2048]{2,1,0:T(8,128)}), f32[3,256,2048]{2,1,0:T(8,128)}) %all-gather.11.cloned.1.call-update) | async-done | bytes 6291472 | tf_op jit(solution)/shard_map/all_gather | solution.py:13
  469.2 32.4 %fusion.7 = f32[4096,2048]{1,0:T(8,128)} fusion(f32[256,512,8]{0,2,1:T(8,128)} %copy.78, f32[3,256,2048]{2,1,0:T(8,128)} %all-gather.11.cloned.1.call-done), kind=kOutput, calls=%fused_computation.8 | convolution fusion | flops 25769803776 | bytes 39845888 | tf_op jit(solution)/shard_map/dot_general | solution.py:29
  501.6 2.7 reduce_sum.28
  504.6 32.4 %fusion.3 = f32[4096,2048]{1,0:T(8,128)} fusion(f32[256,512,8]{0,2,1:T(8,128)} %copy.93, f32[3,256,2048]{2,1,0:T(8,128)} %all-gather.11.cloned.1.call-done), kind=kOutput, calls=%fused_computation.4 | convolution fusion | flops 25769803776 | bytes 39845888 | tf_op jit(solution)/shard_map/dot_general | solution.py:29
  537.0 2.6 reduce_sum.27
  539.9 5.5 copy.108
  545.4 34.0 %fusion.1 = f32[256,2048]{1,0:T(8,128)} fusion(f32[4096,2048]{1,0:T(8,128)} %param.4, f32[256,512,8]{0,2,1:T(8,128)} %copy.108), kind=kOutput, calls=%fused_computation.2 | convolution fusion | flops 25769803776 | bytes 39845888 | tf_op jit(solution)/shard_map/dot_general | solution.py:36
  579.4 0.7 pad_maximum_fusion
  580.1 46.4 %add_add_fusion = f32[4096,2048]{1,0:T(8,128)} fusion(f32[4096,2048]{1,0:T(8,128)} %fusion.7, f32[4096,2048]{1,0:T(8,128)} %fusion.3, f32[256,512,8]{0,2,1:T(8,128)} %copy.108, f32[3,256,2048]{2,1,0:T(8,128)} %all-gather.11.cloned.1.call-done), kind=kOutput, calls=%fused_computation | convolution fusion | flops 25786580992 | bytes 106954752 | tf_op jit(solution)/shard_map/dot_general | solution.py:29
  626.5 1.9 fusion.11
  (68 shorter events, 6.8 us)
Async XLA Ops:
  7.2 86.2 %all-gather.5.cloned.1.call-start = ((), (), s32[]{:S(2)}) async-start(), calls=%async_computation.9 | async-start | bytes 4718592 | tf_op jit(solution)/shard_map/all_gather | solution.py:25
  58.8 117.7 %reduce-scatter.4.cloned.1.call-start = ((), (), s32[]{:S(2)}) async-start(), calls=%async_computation.10 | async-start | bytes 2621440 | tf_op jit(solution)/shard_map/reduce_scatter | solution.py:39
  98.8 33.9 %copy-start.4 = (f32[2048]{0:T(1024)S(1)}, f32[2048]{0:T(1024)}, u32[]{:S(2)}) copy-start(f32[2048]{0:T(1024)} %param.5) | copy-start | bytes 24580
  98.8 77.7 %copy-start.1 = (f32[64,2048]{1,0:T(8,128)S(1)}, f32[64,2048]{1,0:T(8,128)}, u32[]{:S(2)}) copy-start(f32[64,2048]{1,0:T(8,128)} %param.7) | copy-start | bytes 1572868
  132.7 126.3 %all-gather.7.cloned.1.call-start = ((), (), s32[]{:S(2)}) async-start(), calls=%async_computation.11 | async-start | bytes 4718592 | tf_op jit(solution)/shard_map/all_gather | solution.py:25
  224.4 117.7 %reduce-scatter.6.cloned.1.call-start = ((), (), s32[]{:S(2)}) async-start(), calls=%async_computation.12 | async-start | bytes 2621440 | tf_op jit(solution)/shard_map/reduce_scatter | solution.py:39
  264.5 77.7 %copy-start.3 = (f32[64,2048]{1,0:T(8,128)S(1)}, f32[64,2048]{1,0:T(8,128)}, u32[]{:S(2)}) copy-start(f32[64,2048]{1,0:T(8,128)} %reduce-scatter.4.cloned.1.call-done) | copy-start | bytes 1572868
  298.3 43.8 %copy-start = (f32[3,64,2048]{2,1,0:T(8,128)S(1)}, f32[3,64,2048]{2,1,0:T(8,128)}, u32[]{:S(2)}) copy-start(f32[3,64,2048]{2,1,0:T(8,128)} %param.6) | copy-start | bytes 4718596
  298.4 170.9 %all-gather.11.cloned.1.call-start = ((), (), s32[]{:S(2)}) async-start(), calls=%async_computation.15 | async-start | bytes 7864320 | tf_op jit(solution)/shard_map/all_gather | solution.py:13
  299.0 238.0 %all-gather.9.cloned.1.call-start = ((), (), s32[]{:S(2)}) async-start(), calls=%async_computation.13 | async-start | bytes 4718592 | tf_op jit(solution)/shard_map/all_gather | solution.py:25
  408.6 217.9 %reduce-scatter.8.cloned.1.call-start = ((), (), s32[]{:S(2)}) async-start(), calls=%async_computation.14 | async-start | bytes 2621440 | tf_op jit(solution)/shard_map/reduce_scatter | solution.py:39
  580.1 46.4 %copy-start.2 = (f32[64,2048]{1,0:T(8,128)S(1)}, f32[64,2048]{1,0:T(8,128)}, u32[]{:S(2)}) copy-start(f32[64,2048]{1,0:T(8,128)} %get-tuple-element.4) | copy-start | bytes 1572868
Sparse Core Ops, SparseCore 0:
  58.9 34.4 all-gather.4
  132.8 43.6 reduce-scatter.3
  224.5 34.4 all-gather.6
  298.5 43.6 reduce-scatter.5
  343.6 125.6 all-gather.10
  471.0 34.7 all-gather.8
  579.5 41.7 reduce-scatter.7
